TPU v7x, 32 devices: a whole 2x2x4 slice. The times are simulated.
32 devices in a mesh: fsdp: 8 (over z, y), ctx: 2 (over x), tensor: 2 (over core).
Axes of the slice: x: 2, y: 2, z: 4, core: 2. Of those that a mesh axis runs over, the one named last changes fastest.
Arguments:
- block_input: bfloat16 [8, 1024, 1024], P('fsdp', 'ctx'), may hold values from -6 to 6
- operator_gain: bfloat16 [1024], P('fsdp'), may hold values from 0.5 to 1.5
- query_weight: bfloat16 [1024, 1024], P('fsdp', 'tensor'), may hold values from -0.1875 to 0.1875
- key_weight: bfloat16 [1024, 512], P('fsdp', 'tensor'), may hold values from -0.1875 to 0.1875
- value_weight: bfloat16 [1024, 512], P('fsdp', 'tensor'), may hold values from -0.1875 to 0.1875
- output_weight: bfloat16 [1024, 1024], P('tensor', 'fsdp'), may hold values from -0.75 to 0.75
- feedforward_gain: bfloat16 [1024], P('fsdp'), may hold values from 0.5 to 1.5
- gate_weight: bfloat16 [1024, 4608], P('fsdp', 'tensor'), may hold values from -0.1875 to 0.1875
- up_weight: bfloat16 [1024, 4608], P('fsdp', 'tensor'), may hold values from -0.1875 to 0.1875
- down_weight: bfloat16 [4608, 1024], P('tensor', 'fsdp'), may hold values from -0.09375 to 0.09375
- query_gain: bfloat16 [64], P('fsdp'), may hold values from 0.6 to 4
- key_gain: bfloat16 [64], P('fsdp'), may hold values from 0.6 to 4
- cotangent: bfloat16 [8, 1024, 1024], P('fsdp', 'ctx'), may hold values from -6 to 6
Outputs:
- block_output: bfloat16 [8, 1024, 1024], P('fsdp', 'ctx')
- input_grad: float32 [8, 1024, 1024], P('fsdp', 'ctx')
- operator_gain_grad: float32 [1024], P('fsdp')
- query_weight_grad: float32 [1024, 1024], P('fsdp', 'tensor')
- key_weight_grad: float32 [1024, 512], P('fsdp', 'tensor')
- value_weight_grad: float32 [1024, 512], P('fsdp', 'tensor')
- output_weight_grad: float32 [1024, 1024], P('tensor', 'fsdp')
- feedforward_gain_grad: float32 [1024], P('fsdp')
- gate_weight_grad: float32 [1024, 4608], P('fsdp', 'tensor')
- up_weight_grad: float32 [1024, 4608], P('fsdp', 'tensor')
- down_weight_grad: float32 [4608, 1024], P('tensor', 'fsdp')
- query_gain_grad: float32 [64], P('fsdp')
- key_gain_grad: float32 [64], P('fsdp')
All inputs are finite; a program needn't handle non-finite values.
Results may differ from a plain program's by a relative error of at most 0.024.
The roundings to bfloat16 on the way count: a program that leaves them out, or rounds other values in their place, can miss the bound.
Values may be sent and summed in bfloat16 or wider, within the bound.
A program may use at most 192 MiB of HBM per device.

v0:
```python
import jax
import jax.numpy as jnp
from jax import lax
from jax.sharding import PartitionSpec as P

EPS = 1e-05
THETA = 1000000.0


def rms_scale(values_in, gain):
    return (
        values_in * lax.rsqrt(jnp.mean(values_in * values_in, axis=-1, keepdims=True) + EPS) * gain
    )


def rotary_tables(positions, head_width):
    half_width = head_width // 2
    freqs = THETA ** (-jnp.arange(half_width).astype(jnp.float32) * 2.0 / head_width)
    angles = positions.astype(jnp.float32)[:, None] * freqs[None, :]
    return (jnp.cos(angles), jnp.sin(angles))


def rotate_halves(heads_in, cosine, sine):
    half_width = heads_in.shape[-1] // 2
    front_half = heads_in[..., :half_width]
    back_half = heads_in[..., half_width:]
    cos_rows = cosine[:, None, :]
    sin_rows = sine[:, None, :]
    return jnp.concatenate(
        [
            front_half * cos_rows - back_half * sin_rows,
            back_half * cos_rows + front_half * sin_rows,
        ],
        axis=-1,
    )


def head_prepare(raw, gain, cosine, sine):
    head_width = gain.shape[0]
    shaped = raw.reshape(raw.shape[:-1] + (raw.shape[-1] // head_width, head_width))
    return rotate_halves(rms_scale(shaped, gain), cosine, sine)


def swiglu(gate, upper):
    return jax.nn.silu(gate) * upper


def contract(left, right, left_dim, right_dim):
    return lax.dot_general(
        left, right, (((left_dim,), (right_dim,)), ((), ())), preferred_element_type=jnp.float32
    )


def block_scores(query_block, keys, query_pos, key_pos):
    scale = 1.0 / query_block.shape[-1] ** 0.5
    scores = (
        jnp.einsum("qhd,khd->hqk", query_block, keys, preferred_element_type=jnp.float32) * scale
    )
    allowed = key_pos[None, :] <= query_pos[:, None]
    return jnp.where(allowed[None, :, :], scores, -1e30)


def attend(queries, keys, values, positions):
    length = queries.shape[0]
    block_rows = min(512, length)
    outputs = []
    totals = []
    for start in range(0, length, block_rows):
        rows = slice(start, start + block_rows)
        scores = block_scores(queries[rows], keys, positions[rows], positions)
        peak = jnp.max(scores, axis=-1, keepdims=True)
        log_total = peak + jnp.log(jnp.sum(jnp.exp(scores - peak), axis=-1, keepdims=True))
        probs = jnp.exp(scores - log_total).astype(jnp.bfloat16)
        block_out = jnp.einsum("hqk,khd->qhd", probs, values, preferred_element_type=jnp.float32)
        outputs.append(block_out.astype(jnp.bfloat16))
        totals.append(log_total[..., 0])
    return (jnp.concatenate(outputs, axis=0), jnp.concatenate(totals, axis=1))


def attend_grad(queries, keys, values, outputs, totals, out_grad, positions):
    length = queries.shape[0]
    block_rows = min(512, length)
    scale = 1.0 / queries.shape[-1] ** 0.5
    key_acc = jnp.zeros(keys.shape, jnp.float32)
    value_acc = jnp.zeros(values.shape, jnp.float32)
    query_parts = []
    for start in range(0, length, block_rows):
        rows = slice(start, start + block_rows)
        query_block = queries[rows]
        scores = block_scores(query_block, keys, positions[rows], positions)
        probs = jnp.exp(scores - totals[:, rows][..., None])
        grad_block = out_grad[rows]
        value_acc = value_acc + jnp.einsum(
            "hqk,qhd->khd",
            probs.astype(jnp.bfloat16),
            grad_block,
            preferred_element_type=jnp.float32,
        )
        prob_grad = jnp.einsum(
            "qhd,khd->hqk", grad_block, values, preferred_element_type=jnp.float32
        )
        delta = jnp.sum(
            grad_block.astype(jnp.float32) * outputs[rows].astype(jnp.float32), axis=-1
        ).T
        score_grad = (probs * (prob_grad - delta[..., None])).astype(jnp.bfloat16)
        query_parts.append(
            (
                jnp.einsum("hqk,khd->qhd", score_grad, keys, preferred_element_type=jnp.float32)
                * scale
            ).astype(jnp.bfloat16)
        )
        key_acc = (
            key_acc
            + jnp.einsum(
                "hqk,qhd->khd", score_grad, query_block, preferred_element_type=jnp.float32
            )
            * scale
        )
    return (
        jnp.concatenate(query_parts, axis=0),
        key_acc.astype(jnp.bfloat16),
        value_acc.astype(jnp.bfloat16),
    )


def shift(array, axis_name, step):
    size = lax.axis_size(axis_name)
    return lax.ppermute(array, axis_name, [(i, (i + step) % size) for i in range(size)])


def around(array, axis_name, dim):
    size = lax.axis_size(axis_name)
    return jnp.concatenate(
        [array] + [shift(array, axis_name, step) for step in range(1, size)], axis=dim
    )


def group_rows(array):
    return around(around(array, "ctx", 1), "tensor", 1)


def sum_around(array, axis_name):
    size = lax.axis_size(axis_name)
    part = array.shape[1] // size
    total = array[:, :part].astype(jnp.float32)
    for step in range(1, size):
        piece = array[:, step * part : (step + 1) * part].astype(jnp.bfloat16)
        total = total + shift(piece, axis_name, -step).astype(jnp.float32)
    return total


def group_sum(array):
    return sum_around(sum_around(array, "tensor"), "ctx")


def in_order(array, axis_name, dim):
    size = lax.axis_size(axis_name)
    me = lax.axis_index(axis_name)
    width = array.shape[dim]
    shape = list(array.shape)
    shape[dim] = width * size
    out = jnp.zeros(shape, array.dtype)
    for step in range(size):
        piece = array if step == 0 else shift(array, axis_name, step)
        owner = lax.rem(me - step + size, size)
        out = lax.dynamic_update_slice_in_dim(out, piece, owner * width, dim)
    return out


def part_of(array, dim, count, start):
    return lax.dynamic_slice_in_dim(array, start, count, dim)


def shards(
    block_input,
    operator_gain,
    query_weight,
    key_weight,
    value_weight,
    output_weight,
    feedforward_gain,
    gate_weight,
    up_weight,
    down_weight,
    query_gain,
    key_gain,
    cotangent,
):
    bf16 = jnp.bfloat16
    f32 = jnp.float32
    fsdp = lax.axis_size("fsdp")
    ctx = lax.axis_size("ctx")
    tensor = lax.axis_size("tensor")
    me_f = lax.axis_index("fsdp")
    me_c = lax.axis_index("ctx")
    me_t = lax.axis_index("tensor")
    seqs, tok_here, width = block_input.shape
    quarter = tok_here // tensor
    tokens = tok_here * ctx
    rows = seqs * tokens
    gain_rows = query_gain.shape[0]
    head_width = gain_rows * fsdp
    heads_shard = query_weight.shape[1] // head_width
    kv_shard = key_weight.shape[1] // head_width
    spread = heads_shard // kv_shard
    heads = heads_shard // ctx
    kv = max(1, kv_shard // ctx)
    group = heads // kv
    copies = max(1, ctx // kv_shard)
    q_cols = heads * head_width
    kv_cols = kv * head_width
    kv_start = me_c * heads // spread * head_width
    hidden_units = gate_weight.shape[1] // ctx
    shard_rows = query_weight.shape[0]
    gains = jnp.stack(
        [
            operator_gain,
            feedforward_gain,
            jnp.pad(query_gain, (0, shard_rows - gain_rows)),
            jnp.pad(key_gain, (0, shard_rows - gain_rows)),
        ],
        axis=1,
    )
    attention_pack = jnp.concatenate(
        [
            part_of(query_weight, 1, q_cols, me_c * q_cols),
            part_of(key_weight, 1, kv_cols, kv_start),
            part_of(value_weight, 1, kv_cols, kv_start),
            part_of(output_weight, 0, q_cols, me_c * q_cols).T,
            jnp.pad(gains, ((0, 0), (0, 124))),
        ],
        axis=1,
    )
    gate_up_pack = jnp.concatenate(
        [
            part_of(gate_weight, 1, hidden_units, me_c * hidden_units),
            part_of(up_weight, 1, hidden_units, me_c * hidden_units),
        ],
        axis=1,
    )
    down_pack = part_of(down_weight, 0, hidden_units, me_c * hidden_units).T
    attention_full = lax.all_gather(attention_pack, "fsdp", axis=0, tiled=True)
    gate_up_full = lax.all_gather(gate_up_pack, "fsdp", axis=0, tiled=True)
    down_full = lax.all_gather(down_pack, "fsdp", axis=0, tiled=True)
    qkv_cols = q_cols + 2 * kv_cols
    qkv_full = attention_full[:, :qkv_cols]
    output_full = attention_full[:, qkv_cols : qkv_cols + q_cols]
    gains_full = attention_full[:, qkv_cols + q_cols :].astype(f32)
    operator_scale = gains_full[:, 0]
    feedforward_scale = gains_full[:, 1]
    query_scale = gains_full[:, 2].reshape(fsdp, shard_rows)[:, :gain_rows].reshape(-1)
    key_scale = gains_full[:, 3].reshape(fsdp, shard_rows)[:, :gain_rows].reshape(-1)
    own_input = part_of(block_input, 1, quarter, me_t * quarter)
    all_input = group_rows(own_input).reshape(rows, width)
    upstream_own = part_of(cotangent, 1, quarter, me_t * quarter)
    upstream = group_rows(upstream_own).reshape(rows, width)
    ctx_order = lax.rem(me_c - jnp.arange(ctx) + ctx, ctx)
    tensor_order = lax.rem(me_t - jnp.arange(tensor) + tensor, tensor)
    positions = (
        tensor_order[:, None, None] * quarter
        + ctx_order[None, :, None] * tok_here
        + jnp.arange(quarter)[None, None, :]
    ).reshape(tokens)
    cosine, sine = rotary_tables(positions, head_width)

    def prepare(raw, gain):
        return head_prepare(raw, gain, cosine, sine)

    normed_input = rms_scale(all_input.astype(f32), operator_scale).astype(bf16)
    qkv_raw = jnp.dot(normed_input, qkv_full, preferred_element_type=f32).reshape(seqs, tokens, -1)
    query_f32, query_back = jax.vjp(prepare, qkv_raw[..., :q_cols], query_scale)
    key_f32, key_back = jax.vjp(prepare, qkv_raw[..., q_cols : q_cols + kv_cols], key_scale)
    queries = query_f32.astype(bf16)
    keys = jnp.repeat(key_f32.astype(bf16), group, axis=2)
    values = jnp.repeat(
        qkv_raw[..., q_cols + kv_cols :].astype(bf16).reshape(seqs, tokens, kv, head_width),
        group,
        axis=2,
    )
    attended, totals = jax.vmap(attend, in_axes=(0, 0, 0, None))(queries, keys, values, positions)
    attended_rows = attended.reshape(rows, q_cols)
    attention_part = contract(attended_rows, output_full, 1, 1).reshape(seqs, tokens, width)
    own_f32 = own_input.astype(f32)
    hidden = own_f32 + group_sum(attention_part)
    norm_two, norm_two_back = jax.vjp(rms_scale, hidden, feedforward_scale)
    normed_hidden = group_rows(norm_two.astype(bf16)).reshape(rows, width)
    gate_up = jnp.dot(normed_hidden, gate_up_full, preferred_element_type=f32)
    act_f32, act_back = jax.vjp(swiglu, gate_up[:, :hidden_units], gate_up[:, hidden_units:])
    activation = act_f32.astype(bf16)
    act_grad = jnp.dot(upstream, down_full, preferred_element_type=f32)
    gate_grad, up_grad = act_back(act_grad)
    gate_up_grad = jnp.concatenate([gate_grad.astype(bf16), up_grad.astype(bf16)], axis=1)
    hidden_part = contract(gate_up_grad, gate_up_full, 1, 1).reshape(seqs, tokens, width)
    normed_hidden_grad = group_sum(hidden_part)
    down_grad = contract(upstream, activation, 0, 0).astype(bf16)
    down_share = lax.psum_scatter(down_grad, "fsdp", scatter_dimension=0, tiled=True)
    gate_up_weight_grad = contract(normed_hidden, gate_up_grad, 0, 0).astype(bf16)
    gate_up_share = lax.psum_scatter(gate_up_weight_grad, "fsdp", scatter_dimension=0, tiled=True)
    down_part = contract(activation, down_full, 1, 1).reshape(seqs, tokens, width)
    own_output = (hidden + group_sum(down_part)).astype(bf16)
    block_output = in_order(own_output, "tensor", 1)
    hidden_norm_grad, feedforward_gain_grad = norm_two_back(normed_hidden_grad)
    hidden_grad = upstream_own.astype(f32) + hidden_norm_grad
    hidden_grad_b = group_rows(hidden_grad.astype(bf16)).reshape(rows, width)
    output_weight_grad = contract(hidden_grad_b, attended_rows, 0, 0)
    attended_grad = (
        jnp.dot(hidden_grad_b, output_full, preferred_element_type=f32)
        .astype(bf16)
        .reshape(seqs, tokens, heads, head_width)
    )
    query_hgrad, key_hgrad, value_hgrad = jax.vmap(attend_grad, in_axes=(0, 0, 0, 0, 0, 0, None))(
        queries, keys, values, attended, totals, attended_grad, positions
    )

    def head_sum(grad):
        return grad.astype(f32).reshape(seqs, tokens, kv, group, head_width).sum(axis=3)

    query_pre, query_gain_grad = query_back(query_hgrad.astype(f32))
    key_pre, key_gain_grad = key_back(head_sum(key_hgrad))
    qkv_raw_grad = jnp.concatenate(
        [
            query_pre.astype(bf16).reshape(rows, q_cols),
            key_pre.astype(bf16).reshape(rows, kv_cols),
            head_sum(value_hgrad).astype(bf16).reshape(rows, kv_cols),
        ],
        axis=1,
    )
    input_part = contract(qkv_raw_grad, qkv_full, 1, 1).reshape(seqs, tokens, width)
    normed_input_grad = group_sum(input_part)
    qkv_weight_grad = contract(normed_input, qkv_raw_grad, 0, 0)
    attention_grad = jnp.concatenate([qkv_weight_grad, output_weight_grad], axis=1).astype(bf16)
    attention_share = lax.psum_scatter(attention_grad, "fsdp", scatter_dimension=0, tiled=True)
    _, norm_one_back = jax.vjp(rms_scale, own_f32, operator_scale)
    input_norm_grad, operator_gain_grad = norm_one_back(normed_input_grad)
    input_grad = in_order(hidden_grad + input_norm_grad, "tensor", 1)
    gain_sums = lax.psum(
        jnp.concatenate(
            [operator_gain_grad, feedforward_gain_grad, query_gain_grad, key_gain_grad]
        ),
        ("fsdp", "ctx", "tensor"),
    )
    operator_share = part_of(gain_sums, 0, shard_rows, me_f * shard_rows)
    feedforward_share = part_of(gain_sums, 0, shard_rows, width + me_f * shard_rows)
    query_gain_share = part_of(gain_sums, 0, gain_rows, 2 * width + me_f * gain_rows)
    key_gain_share = part_of(gain_sums, 0, gain_rows, 2 * width + head_width + me_f * gain_rows)

    def spread_cols(share):
        return in_order(share, "ctx", 1).astype(f32)

    def spread_heads(share):
        if copies == 1:
            return spread_cols(share)
        every = in_order(share, "ctx", 1).astype(f32)
        return (
            every.reshape(shard_rows, kv_shard, copies, head_width)
            .sum(axis=2)
            .reshape(shard_rows, -1)
        )

    return (
        block_output,
        input_grad,
        operator_share,
        spread_cols(attention_share[:, :q_cols]),
        spread_heads(attention_share[:, q_cols : q_cols + kv_cols]),
        spread_heads(attention_share[:, q_cols + kv_cols : qkv_cols]),
        in_order(attention_share[:, qkv_cols:].T, "ctx", 0).astype(f32),
        feedforward_share,
        spread_cols(gate_up_share[:, :hidden_units]),
        spread_cols(gate_up_share[:, hidden_units:]),
        in_order(down_share.T, "ctx", 0).astype(f32),
        query_gain_share,
        key_gain_share,
    )


def solution(mesh):
    in_specs = (
        P("fsdp", "ctx", None),
        P("fsdp"),
        P("fsdp", "tensor"),
        P("fsdp", "tensor"),
        P("fsdp", "tensor"),
        P("tensor", "fsdp"),
        P("fsdp"),
        P("fsdp", "tensor"),
        P("fsdp", "tensor"),
        P("tensor", "fsdp"),
        P("fsdp"),
        P("fsdp"),
        P("fsdp", "ctx", None),
    )
    out_specs = (
        P("fsdp", "ctx", None),
        P("fsdp", "ctx", None),
        P("fsdp"),
        P("fsdp", "tensor"),
        P("fsdp", "tensor"),
        P("fsdp", "tensor"),
        P("tensor", "fsdp"),
        P("fsdp"),
        P("fsdp", "tensor"),
        P("fsdp", "tensor"),
        P("tensor", "fsdp"),
        P("fsdp"),
        P("fsdp"),
    )
    return jax.shard_map(shards, mesh=mesh, in_specs=in_specs, out_specs=out_specs, check_vma=False)
```

profile of v0, /device:TPU:0, one launch (start us, length us, event | category | flops | bytes accessed | tf_op | source)
XLA Modules:
  0.0 509.7 jit_solution(16331534721619559554)
XLA Ops:
  18.8 9.8 %collective-permute-done = bf16[1,256,1024]{2,1,0:T(8,128)(2,1)S(1)} collective-permute-done((bf16[1,256,1024]{2,1,0:T(8,128)(2,1)S(1)}, bf16[1,256,1024]{2,1,0:T(8,128)(2,1)S(1)}, u32[]{:S(2)}, u32[]{:S(2)}) %collective-permute-start) | collective-permute-done | bytes 524320 | tf_op jit(solution)/shard_map/ppermute | solution.py:128
  31.9 31.1 %all-gather.4.cloned.1.call-done = bf16[1024,896]{0,1:T(8,128)(2,1)} async-done(((bf16[128,896]{0,1:T(8,128)(2,1)}), bf16[1024,896]{0,1:T(8,128)(2,1)}) %all-gather.4.cloned.1.call-update) | async-done | bytes 1835024 | tf_op jit(solution)/shard_map/all_gather | solution.py:242
  64.1 3.1 convolution_bitcast_fusion.3
  99.4 12.4 %collective-permute-done.3 = bf16[1,256,1024]{2,1,0:T(8,128)(2,1)S(1)} collective-permute-done((bf16[1,256,1024]{2,1,0:T(8,128)(2,1)S(1)}, bf16[1,256,1024]{2,1,0:T(8,128)(2,1)S(1)}, u32[]{:S(2)}, u32[]{:S(2)}) %collective-permute-start.3) | collective-permute-done | bytes 524320 | tf_op jit(solution)/shard_map/ppermute | solution.py:128
  113.9 11.7 %collective-permute-done.4 = bf16[1,256,1024]{2,1,0:T(8,128)(2,1)S(1)} collective-permute-done((bf16[1,256,1024]{2,1,0:T(8,128)(2,1)S(1)}, bf16[1,256,1024]{2,1,0:T(8,128)(2,1)S(1)}, u32[]{:S(2)}, u32[]{:S(2)}) %collective-permute-start.4) | collective-permute-done | bytes 524320 | tf_op jit(solution)/shard_map/ppermute | solution.py:128
  128.1 12.8 %collective-permute-done.9 = bf16[1,256,1024]{2,1,0:T(8,128)(2,1)S(1)} collective-permute-done((bf16[1,256,1024]{2,1,0:T(8,128)(2,1)S(1)}, bf16[1,256,1024]{2,1,0:T(8,128)(2,1)S(1)}, u32[]{:S(2)}, u32[]{:S(2)}) %collective-permute-start.9) | collective-permute-done | bytes 524320 | tf_op jit(solution)/shard_map/ppermute | solution.py:128
  143.3 11.5 %fusion.36 = f32[1024,2304]{1,0:T(8,128)} fusion(bf16[1024,2304]{1,0:T(8,128)(2,1)} %all-gather.6.cloned.1.call-done, bf16[1,512,1024]{2,1,0:T(8,128)(2,1)} %collective-permute-done.5, bf16[1,256,1024]{2,1,0:T(8,128)(2,1)} %copy-done.49, bf16[1,256,1024]{2,1,0:T(8,128)(2,1)S(1)} %multiply_convert_fusion.4), kind=kOutput, calls=%fused_computation.111 | convolution fusion | flops 4838129664 | bytes 16252928 | tf_op jit(solution)/shard_map/dot_general | solution.py:287
  154.9 42.4 %all-gather.8.cloned.1.call-done = bf16[1024,1152]{0,1:T(8,128)(2,1)} async-done(((bf16[128,1152]{0,1:T(8,128)(2,1)}), bf16[1024,1152]{0,1:T(8,128)(2,1)}) %all-gather.8.cloned.1.call-update) | async-done | bytes 2359312 | tf_op jit(solution)/shard_map/all_gather | solution.py:244
  197.3 9.1 %fusion.6 = (bf16[1024,1152]{1,0:T(8,128)(2,1)S(1)}, bf16[1024,1152]{1,0:T(8,128)(2,1)S(1)}, bf16[1024,1152]{1,0:T(8,128)(2,1)S(1)}) fusion(f32[1024,2304]{1,0:T(8,128)} %fusion.36, bf16[1024,1152]{0,1:T(8,128)(2,1)} %all-gather.8.cloned.1.call-done, bf16[1,512,1024]{2,1,0:T(8,128)(2,1)} %collective-permute-done.10, bf16[1,256,1024]{2,1,0:T(8,128)(2,1)} %copy-done.53, ...), kind=kOutput, calls=%fused_computation.18 | convolution fusion | flops 2441084928 | bytes 20971520 | tf_op jit(solution)/shard_map/dot_general | solution.py:290
  206.4 5.1 fusion.12
  216.3 12.5 %collective-permute-done.12 = bf16[1,256,1024]{2,1,0:T(8,128)(2,1)S(1)} collective-permute-done((bf16[1,256,1024]{2,1,0:T(8,128)(2,1)S(1)}, bf16[1,256,1024]{2,1,0:T(8,128)(2,1)S(1)}, u32[]{:S(2)}, u32[]{:S(2)}) %collective-permute-start.12) | collective-permute-done | bytes 524320 | tf_op jit(solution)/shard_map/ppermute | solution.py:128
  232.1 11.6 %collective-permute-done.13 = bf16[1,256,1024]{2,1,0:T(8,128)(2,1)S(1)} collective-permute-done((bf16[1,256,1024]{2,1,0:T(8,128)(2,1)S(1)}, bf16[1,256,1024]{2,1,0:T(8,128)(2,1)S(1)}, u32[]{:S(2)}, u32[]{:S(2)}) %collective-permute-start.13) | collective-permute-done | bytes 524320 | tf_op jit(solution)/shard_map/ppermute | solution.py:128
  245.6 5.6 %convolution_convert_fusion.1 = bf16[1024,1152]{1,0:T(8,128)(2,1)} fusion(bf16[1024,1152]{1,0:T(8,128)(2,1)S(1)} %get-tuple-element.35, bf16[1,512,1024]{2,1,0:T(8,128)(2,1)} %collective-permute-done.10, bf16[1,256,1024]{2,1,0:T(8,128)(2,1)S(1)} %copy-done.54, bf16[1,256,1024]{2,1,0:T(8,128)(2,1)S(1)} %constant_dynamic-slice_fusion), kind=kOutput, calls=%fused_computation.27 | convolution fusion | flops 2423390208 | bytes 6815744 | tf_op jit(solution)/shard_map/dot_general | solution.py:49
  254.2 5.5 %multiply_convert_fusion.1 = bf16[4,512,1024]{2,1,0:T(8,128)(2,1)S(1)} fusion(f32[4,512,1024]{2,1,0:T(8,128)} %copy-done.2, f32[4,512]{1,0:T(4,128)S(1)} %bitcast.212, f32[4,512]{1,0:T(4,128)S(1)} %log_add_fusion.1, pred[512,1024]{1,0:T(8,128)(4,1)S(1)} %copy-done.14, bf16[1024,4,64]{0,2,1:T(8,128)(2,1)S(1)} %bitcast.186, ...), kind=kOutput, calls=%fused_computation.1 | convolution fusion | flops 281018368 | bytes 13910016 | tf_op jit(solution)/shard_map/vmap(qhd,khd->hqk)/dot_general | solution.py:99
  259.8 3.5 multiply_convert_fusion
  270.7 3.8 fusion.22
  290.6 10.1 %convolution_convert_fusion = bf16[1024,2304]{1,0:T(8,128)(2,1)} fusion(bf16[1024,1152]{1,0:T(8,128)(2,1)} %copy-done.66, bf16[1024,1152]{1,0:T(8,128)(2,1)} %copy-done.65, bf16[1,512,1024]{2,1,0:T(8,128)(2,1)} %collective-permute-done.5, bf16[1,256,1024]{2,1,0:T(8,128)(2,1)S(1)} %copy-done.50, bf16[1,256,1024]{2,1,0:T(8,128)(2,1)S(1)} %copy-done.31), kind=kOutput, calls=%fused_computation.11 | convolution fusion | flops 4849926144 | bytes 11534336 | tf_op jit(solution)/shard_map/dot_general | solution.py:49
  300.7 5.4 %convolution_bitcast_fusion.2 = f32[1,1024,1024]{2,1,0:T(8,128)S(1)} fusion(bf16[1024,1152]{1,0:T(8,128)(2,1)} %copy-done.67, bf16[1024,1152]{0,1:T(8,128)(2,1)} %all-gather.8.cloned.1.call-done), kind=kOutput, calls=%fused_computation.32 | convolution fusion | flops 2415919104 | bytes 8912896 | tf_op jit(solution)/shard_map/dot_general | solution.py:49
  318.7 12.0 %collective-permute-done.7 = bf16[1,256,1024]{2,1,0:T(8,128)(2,1)S(1)} collective-permute-done((bf16[1,256,1024]{2,1,0:T(8,128)(2,1)S(1)}, bf16[1,256,1024]{2,1,0:T(8,128)(2,1)S(1)}, u32[]{:S(2)}, u32[]{:S(2)}) %collective-permute-start.7) | collective-permute-done | bytes 524320 | tf_op jit(solution)/shard_map/ppermute | solution.py:128
  332.0 9.5 %collective-permute-done.16 = bf16[1,256,1024]{2,1,0:T(8,128)(2,1)S(1)} collective-permute-done((bf16[1,256,1024]{2,1,0:T(8,128)(2,1)S(1)}, bf16[1,256,1024]{2,1,0:T(8,128)(2,1)S(1)}, u32[]{:S(2)}, u32[]{:S(2)}) %collective-permute-start.16) | collective-permute-done | bytes 524320 | tf_op jit(solution)/shard_map/ppermute | solution.py:128
  348.2 40.7 %psum.7 = f32[2176]{0:T(1024)S(1)} all-reduce(f32[2176]{0:T(1024)S(1)} %concatenate.102), channel_id=1, replica_groups=mesh['fsdp'=8,'ctx'=2,'tensor'=2] {'fsdp','ctx','tensor'}, use_global_device_ids=true, to_apply=%region_21.22 | all-reduce | flops 2176 | bytes 17408 | tf_op jit(solution)/shard_map/psum | solution.py:336
  405.0 80.4 %reduce-scatter.6.cloned.1.call-done = bf16[128,2304]{1,0:T(8,128)(2,1)} async-done(((bf16[1024,2304]{1,0:T(8,128)(2,1)}), bf16[128,2304]{1,0:T(8,128)(2,1)}) %reduce-scatter.6.cloned.1.call-update) | async-done | bytes 589840 | tf_op jit(solution)/shard_map/reduce_scatter | solution.py:298
  489.7 6.8 %collective-permute-done.23 = bf16[128,1152]{1,0:T(8,128)(2,1)S(1)} collective-permute-done((bf16[128,1152]{1,0:T(8,128)(2,1)S(1)}, bf16[128,1152]{1,0:T(8,128)(2,1)S(1)}, u32[]{:S(2)}, u32[]{:S(2)}) %collective-permute-start.23) | collective-permute-done | bytes 294944 | tf_op jit(solution)/shard_map/ppermute | solution.py:128
  497.7 3.8 collective-permute-done.22
  (356 shorter events, 133.5 us)
Async XLA Ops:
  7.2 55.8 %all-gather.4.cloned.1.call-start = ((), (), s32[]{:S(2)}) async-start(), calls=%async_computation.3 | async-start | bytes 2064384 | tf_op jit(solution)/shard_map/all_gather | solution.py:242
  12.5 130.9 %all-gather.6.cloned.1.call-start = ((), (), s32[]{:S(2)}) async-start(), calls=%async_computation.4 | async-start | bytes 5308416 | tf_op jit(solution)/shard_map/all_gather | solution.py:243
  13.8 14.9 %collective-permute-start = (bf16[1,256,1024]{2,1,0:T(8,128)(2,1)S(1)}, bf16[1,256,1024]{2,1,0:T(8,128)(2,1)S(1)}, u32[]{:S(2)}, u32[]{:S(2)}) collective-permute-start(bf16[1,256,1024]{2,1,0:T(8,128)(2,1)S(1)} %get-tuple-element.28), channel_id=1, source_target_pairs={{0,2},{2,0},{1,3},{3,1},{4,6},{6,4},{5,7},{7,5},{8,10},{10,8},{9,1... | collective-permute-start | bytes 1572872 | tf_op jit(solution)/shard_map/ppermute | solution.py:128
  18.7 178.6 %all-gather.8.cloned.1.call-start = ((), (), s32[]{:S(2)}) async-start(), calls=%async_computation.5 | async-start | bytes 2654208 | tf_op jit(solution)/shard_map/all_gather | solution.py:244
  93.7 251.7 %reduce-scatter.8.cloned.1.call-start = ((), (), s32[]{:S(2)}) async-start(), calls=%async_computation.7 | async-start | bytes 2654208 | tf_op jit(solution)/shard_map/reduce_scatter | solution.py:296
  97.8 14.0 %collective-permute-start.3 = (bf16[1,256,1024]{2,1,0:T(8,128)(2,1)S(1)}, bf16[1,256,1024]{2,1,0:T(8,128)(2,1)S(1)}, u32[]{:S(2)}, u32[]{:S(2)}) collective-permute-start(bf16[1,256,1024]{2,1,0:T(8,128)(2,1)S(1)} %slice.359), channel_id=1, source_target_pairs={{0,2},{2,0},{1,3},{3,1},{4,6},{6,4},{5,7},{7,5},{8,10},{10,8},{9,1... | collective-permute-start | bytes 1572872 | tf_op jit(solution)/shard_map/ppermute | solution.py:128
  112.3 13.3 %collective-permute-start.4 = (bf16[1,256,1024]{2,1,0:T(8,128)(2,1)S(1)}, bf16[1,256,1024]{2,1,0:T(8,128)(2,1)S(1)}, u32[]{:S(2)}, u32[]{:S(2)}) collective-permute-start(bf16[1,256,1024]{2,1,0:T(8,128)(2,1)S(1)} %multiply_convert_fusion.4), channel_id=1, source_target_pairs={{0,2},{2,0},{1,3},{3,1},{4,6},{6,4},{5,7},{7,5},{8,10},{10,8},{9,1... | collective-permute-start | bytes 1572872 | tf_op jit(solution)/shard_map/ppermute | solution.py:128
  126.4 16.3 %collective-permute-start.5 = (bf16[1,512,1024]{2,1,0:T(8,128)(2,1)S(1)}, bf16[1,512,1024]{2,1,0:T(8,128)(2,1)}, u32[]{:S(2)}, u32[]{:S(2)}) collective-permute-start(bf16[1,512,1024]{2,1,0:T(8,128)(2,1)S(1)} %pad_maximum_fusion.7), channel_id=1, source_target_pairs={{0,1},{1,0},{2,3},{3,2},{4,5},{5,4},{6,7},{7,6},{8,9},{9,8},{10,11... | collective-permute-start | bytes 3145736 | tf_op jit(solution)/shard_map/ppermute | solution.py:128
  126.5 14.4 %collective-permute-start.9 = (bf16[1,256,1024]{2,1,0:T(8,128)(2,1)S(1)}, bf16[1,256,1024]{2,1,0:T(8,128)(2,1)S(1)}, u32[]{:S(2)}, u32[]{:S(2)}) collective-permute-start(bf16[1,256,1024]{2,1,0:T(8,128)(2,1)S(1)} %constant_dynamic-slice_fusion), channel_id=1, source_target_pairs={{0,2},{2,0},{1,3},{3,1},{4,6},{6,4},{5,7},{7,5},{8,10},{10,8},{9,1... | collective-permute-start | bytes 1572872 | tf_op jit(solution)/shard_map/ppermute | solution.py:128
  142.7 12.2 %collective-permute-start.10 = (bf16[1,512,1024]{2,1,0:T(8,128)(2,1)}, bf16[1,512,1024]{2,1,0:T(8,128)(2,1)}, u32[]{:S(2)}, u32[]{:S(2)}) collective-permute-start(bf16[1,512,1024]{2,1,0:T(8,128)(2,1)} %pad_maximum_fusion.8), channel_id=1, source_target_pairs={{0,1},{1,0},{2,3},{3,2},{4,5},{5,4},{6,7},{7,6},{8,9},{9,8},{10,11... | collective-permute-start | bytes 3145736 | tf_op jit(solution)/shard_map/ppermute | solution.py:128
  214.8 14.0 %collective-permute-start.12 = (bf16[1,256,1024]{2,1,0:T(8,128)(2,1)S(1)}, bf16[1,256,1024]{2,1,0:T(8,128)(2,1)S(1)}, u32[]{:S(2)}, u32[]{:S(2)}) collective-permute-start(bf16[1,256,1024]{2,1,0:T(8,128)(2,1)S(1)} %slice.357), channel_id=1, source_target_pairs={{0,2},{2,0},{1,3},{3,1},{4,6},{6,4},{5,7},{7,5},{8,10},{10,8},{9,1... | collective-permute-start | bytes 1572872 | tf_op jit(solution)/shard_map/ppermute | solution.py:128
  230.6 13.1 %collective-permute-start.13 = (bf16[1,256,1024]{2,1,0:T(8,128)(2,1)S(1)}, bf16[1,256,1024]{2,1,0:T(8,128)(2,1)S(1)}, u32[]{:S(2)}, u32[]{:S(2)}) collective-permute-start(bf16[1,256,1024]{2,1,0:T(8,128)(2,1)S(1)} %get-tuple-element.25), channel_id=1, source_target_pairs={{0,2},{2,0},{1,3},{3,1},{4,6},{6,4},{5,7},{7,5},{8,10},{10,8},{9,1... | collective-permute-start | bytes 1572872 | tf_op jit(solution)/shard_map/ppermute | solution.py:128
  245.6 5.8 %collective-permute-start.14 = (bf16[1,512,1024]{2,1,0:T(8,128)(2,1)}, bf16[1,512,1024]{2,1,0:T(8,128)(2,1)}, u32[]{:S(2)}, u32[]{:S(2)}) collective-permute-start(bf16[1,512,1024]{2,1,0:T(8,128)(2,1)} %pad_maximum_fusion.9), channel_id=1, source_target_pairs={{0,1},{1,0},{2,3},{3,2},{4,5},{5,4},{6,7},{7,6},{8,9},{9,8},{10,11... | collective-permute-start | bytes 3145736 | tf_op jit(solution)/shard_map/ppermute | solution.py:128
  251.3 141.6 %reduce-scatter.10.cloned.1.call-start = ((), (), s32[]{:S(2)}) async-start(), calls=%async_computation.8 | async-start | bytes 1769472
  290.3 195.1 %reduce-scatter.6.cloned.1.call-start = ((), (), s32[]{:S(2)}) async-start(), calls=%async_computation.6 | async-start | bytes 5308416 | tf_op jit(solution)/shard_map/reduce_scatter | solution.py:298
  308.4 5.0 collective-permute-start.6
  315.9 14.9 %collective-permute-start.7 = (bf16[1,256,1024]{2,1,0:T(8,128)(2,1)S(1)}, bf16[1,256,1024]{2,1,0:T(8,128)(2,1)S(1)}, u32[]{:S(2)}, u32[]{:S(2)}) collective-permute-start(bf16[1,256,1024]{2,1,0:T(8,128)(2,1)S(1)} %slice.358), channel_id=1, source_target_pairs={{0,2},{2,0},{1,3},{3,1},{4,6},{6,4},{5,7},{7,5},{8,10},{10,8},{9,1... | collective-permute-start | bytes 1572872 | tf_op jit(solution)/shard_map/ppermute | solution.py:128
  318.0 23.5 %collective-permute-start.16 = (bf16[1,256,1024]{2,1,0:T(8,128)(2,1)S(1)}, bf16[1,256,1024]{2,1,0:T(8,128)(2,1)S(1)}, u32[]{:S(2)}, u32[]{:S(2)}) collective-permute-start(bf16[1,256,1024]{2,1,0:T(8,128)(2,1)S(1)} %slice.356), channel_id=1, source_target_pairs={{0,2},{2,0},{1,3},{3,1},{4,6},{6,4},{5,7},{7,5},{8,10},{10,8},{9,1... | collective-permute-start | bytes 1572872 | tf_op jit(solution)/shard_map/ppermute | solution.py:128
  331.9 11.6 %collective-permute-start.8 = (bf16[1,256,1024]{2,1,0:T(8,128)(2,1)}, bf16[1,256,1024]{2,1,0:T(8,128)(2,1)}, u32[]{:S(2)}, u32[]{:S(2)}) collective-permute-start(bf16[1,256,1024]{2,1,0:T(8,128)(2,1)} %get-tuple-element.30), channel_id=1, source_target_pairs={{0,1},{1,0},{2,3},{3,2},{4,5},{5,4},{6,7},{7,6},{8,9},{9,8},{10,11... | collective-permute-start | bytes 1572872 | tf_op jit(solution)/shard_map/ppermute | solution.py:128
  343.5 48.0 %collective-permute-start.17 = (f32[1,256,1024]{2,1,0:T(8,128)}, f32[1,256,1024]{2,1,0:T(8,128)}, u32[]{:S(2)}, u32[]{:S(2)}) collective-permute-start(f32[1,256,1024]{2,1,0:T(8,128)} %get-tuple-element.24), channel_id=1, source_target_pairs={{0,1},{1,0},{2,3},{3,2},{4,5},{5,4},{6,7},{7,6},{8,9},{9,8},{10,11... | collective-permute-start | bytes 3145736 | tf_op jit(solution)/shard_map/ppermute | solution.py:128
  346.6 43.6 %collective-permute-start.24 = (bf16[1152,128]{0,1:T(8,128)(2,1)}, bf16[1152,128]{0,1:T(8,128)(2,1)S(1)}, u32[]{:S(2)}, u32[]{:S(2)}) collective-permute-start(bf16[1152,128]{0,1:T(8,128)(2,1)} %bitcast.196), channel_id=1, source_target_pairs={{0,2},{2,0},{1,3},{3,1},{4,6},{6,4},{5,7},{7,5},{8,10},{10,8},{9,1... | collective-permute-start | bytes 884744 | tf_op jit(solution)/shard_map/ppermute | solution.py:128
  394.1 8.9 %collective-permute-start.21 = (bf16[256,128]{1,0:T(8,128)(2,1)S(1)}, bf16[256,128]{1,0:T(8,128)(2,1)S(1)}, u32[]{:S(2)}, u32[]{:S(2)}) collective-permute-start(bf16[256,128]{1,0:T(8,128)(2,1)S(1)} %bitcast.199), channel_id=1, source_target_pairs={{0,2},{2,0},{1,3},{3,1},{4,6},{6,4},{5,7},{7,5},{8,10},{10,8},{9,1... | collective-permute-start | bytes 196616 | tf_op jit(solution)/shard_map/ppermute | solution.py:128
  486.6 9.9 %collective-permute-start.23 = (bf16[128,1152]{1,0:T(8,128)(2,1)S(1)}, bf16[128,1152]{1,0:T(8,128)(2,1)S(1)}, u32[]{:S(2)}, u32[]{:S(2)}) collective-permute-start(bf16[128,1152]{1,0:T(8,128)(2,1)S(1)} %get-tuple-element.44), channel_id=1, source_target_pairs={{0,2},{2,0},{1,3},{3,1},{4,6},{6,4},{5,7},{7,5},{8,10},{10,8},{9,1... | collective-permute-start | bytes 884744 | tf_op jit(solution)/shard_map/ppermute | solution.py:128
  488.1 13.3 %collective-permute-start.22 = (bf16[128,1152]{1,0:T(8,128)(2,1)S(1)}, bf16[128,1152]{1,0:T(8,128)(2,1)S(1)}, u32[]{:S(2)}, u32[]{:S(2)}) collective-permute-start(bf16[128,1152]{1,0:T(8,128)(2,1)S(1)} %get-tuple-element.46), channel_id=1, source_target_pairs={{0,2},{2,0},{1,3},{3,1},{4,6},{6,4},{5,7},{7,5},{8,10},{10,8},{9,1... | collective-permute-start | bytes 884744 | tf_op jit(solution)/shard_map/ppermute | solution.py:128
  (81 other events, 918.0 us)
Sparse Core Ops, SparseCore 0:
  12.6 50.3 all-gather.3
  65.8 77.4 all-gather.5
  145.4 51.8 all-gather.7
  251.4 67.9 reduce-scatter.7
  322.6 64.6 reduce-scatter.9
  390.8 94.5 reduce-scatter.5
where the time goes:
time: 516 us; the launch traced here: 510 us
  waiting for transfers between devices  264 us (51%)
  matrix products  89.8 us (17%)
  blocking collectives  40.7 us (8%)
  other arithmetic  38.9 us (8%)
  local copies, waits for them, and re-layouts  38.3 us (7%)
  starting transfers between devices  22.3 us (4%)
  between operations  15.9 us (3%)
    ppermute x25, waiting for transfers between devices, shift(): lax.ppermute(array, axis_name, [(i, (i + step) % size) for i in range(siz...  109 us
    reduce_scatter x1, waiting for transfers between devices, shards(): lax.psum_scatter(gate_up_weight_grad, 'fsdp', scatter_dimension=0, tiled=...  80.4 us
    all_gather x1, waiting for transfers between devices, shards(): down_full = lax.all_gather(down_pack, 'fsdp', axis=0, tiled=True)  42.4 us
    psum x1, blocking collectives, shards(): lax.psum(jnp.concatenate([operator_gain_grad, feedforward_gain_grad, quer...  40.7 us
    dot_general x8, matrix products, contract(): lax.dot_general(left, right, (((left_dim,), (right_dim,)), ((), ())), pre...  33.3 us
    all_gather x1, waiting for transfers between devices, shards(): attention_full = lax.all_gather(attention_pack, 'fsdp', axis=0, tiled=True)  31.1 us
    ppermute x25, starting transfers between devices, shift(): lax.ppermute(array, axis_name, [(i, (i + step) % size) for i in range(siz...  21.9 us
    unnamed x164, local copies, waits for them, and re-layouts  15.2 us
  transfers between devices with their start and end apart: 31, of which 19 were waited for; matrix products, arithmetic and copies ran while one was open for 26% of the time, Pallas kernels for 0%

commit v1 on v0

--- a/solution.py
+++ b/solution.py
@@ -239,7 +239,18 @@
         axis=1,
     )
     down_pack = part_of(down_weight, 0, hidden_units, me_c * hidden_units).T
-    attention_full = lax.all_gather(attention_pack, "fsdp", axis=0, tiled=True)
+    ways = lax.axis_size("fsdp")
+    up = [(d, (d + 1) % ways) for d in range(ways)]
+    down = [(d, (d - 1) % ways) for d in range(ways)]
+    earlier, later = ([attention_pack], [attention_pack])
+    for _ in range(ways // 2):
+        earlier.append(lax.ppermute(earlier[-1], "fsdp", up))
+    for _ in range((ways - 1) // 2):
+        later.append(lax.ppermute(later[-1], "fsdp", down))
+    line = jnp.concatenate([*earlier[::-1], *later[1:]], axis=0)
+    attention_full = jnp.roll(
+        line, (lax.axis_index("fsdp") - ways // 2) * attention_pack.shape[0], axis=0
+    )
     gate_up_full = lax.all_gather(gate_up_pack, "fsdp", axis=0, tiled=True)
     down_full = lax.all_gather(down_pack, "fsdp", axis=0, tiled=True)
     qkv_cols = q_cols + 2 * kv_cols

time: 516 us -> 484 us (0.938)
  waiting for transfers between devices: 264 us -> 206 us
  starting transfers between devices: 22.3 us -> 39.6 us
  local copies, waits for them, and re-layouts: 38.3 us -> 45.5 us
    all_gather x1, waiting for transfers between devices: 42.4 us -> 1.75 us  [shards(): down_full = lax.all_gather(down_pack, 'fsdp', axis=0, tiled=True)]
    all_gather x1 -> x0, waiting for transfers between devices: 31.1 us -> none  [shards(): attention_full = lax.all_gather(attention_pack, 'fsdp', axis=0, tiled=True)]
    ppermute x0 -> x7, waiting for transfers between devices: none -> 25.5 us  [the longest x4 25.5 us: shards(): earlier.append(lax.ppermute(earlier[-1], 'fsdp', up))]
    ppermute x0 -> x7, starting transfers between devices: none -> 19.2 us  [the longest x3 11.6 us: shards(): later.append(lax.ppermute(later[-1], 'fsdp', down))]
    unnamed x164 -> x183, local copies, waits for them, and re-layouts: 15.2 us -> 24.9 us
    ppermute x25, waiting for transfers between devices: 109 us -> 99.4 us  [shift(): lax.ppermute(array, axis_name, [(i, (i + step) % size) for i in range(siz...]
  transfers between devices with their start and end apart: 31 -> 37, of which waited for: 19 -> 19; matrix products, arithmetic and copies ran while one was open for 26% -> 29% of each run, Pallas kernels for 0% -> 0%
where the time goes in v1:
time: 484 us; the launch traced here: 476 us
  waiting for transfers between devices  206 us (43%)
  matrix products  91.7 us (19%)
  local copies, waits for them, and re-layouts  45.5 us (9%)
  blocking collectives  41.5 us (9%)
  starting transfers between devices  39.6 us (8%)
  other arithmetic  36.4 us (8%)
  between operations  15.8 us (3%)
    ppermute x25, waiting for transfers between devices, shift(): lax.ppermute(array, axis_name, [(i, (i + step) % size) for i in range(siz...  99.4 us
    reduce_scatter x1, waiting for transfers between devices, shards(): lax.psum_scatter(gate_up_weight_grad, 'fsdp', scatter_dimension=0, tiled=...  78.8 us
    psum x1, blocking collectives, shards(): lax.psum(jnp.concatenate([operator_gain_grad, feedforward_gain_grad, quer...  41.5 us
    dot_general x8, matrix products, contract(): lax.dot_general(left, right, (((left_dim,), (right_dim,)), ((), ())), pre...  35.2 us
    ppermute x4, waiting for transfers between devices, shards(): earlier.append(lax.ppermute(earlier[-1], 'fsdp', up))  25.5 us
    unnamed x183, local copies, waits for them, and re-layouts  24.9 us
    ppermute x25, starting transfers between devices, shift(): lax.ppermute(array, axis_name, [(i, (i + step) % size) for i in range(siz...  20 us
    ppermute x3, starting transfers between devices, shards(): later.append(lax.ppermute(later[-1], 'fsdp', down))  11.6 us
  transfers between devices with their start and end apart: 37, of which 19 were waited for; matrix products, arithmetic and copies ran while one was open for 29% of the time, Pallas kernels for 0%

profile of v1, /device:TPU:0, one launch (start us, length us, event | category | flops | bytes accessed | tf_op | source)
XLA Modules:
  0.0 476.1 jit_solution(2632232070321642448)
XLA Ops:
  27.1 8.6 %collective-permute-done.3 = bf16[128,896]{0,1:T(8,128)(2,1)S(1)} collective-permute-done((bf16[128,896]{0,1:T(8,128)(2,1)S(1)}, bf16[128,896]{0,1:T(8,128)(2,1)S(1)}, u32[]{:S(2)}, u32[]{:S(2)}) %collective-permute-start.3) | collective-permute-done | bytes 229408 | tf_op jit(solution)/shard_map/ppermute | solution.py:247
  38.4 3.7 collective-permute-start.7
  42.1 9.3 %collective-permute-done.4 = bf16[128,896]{0,1:T(8,128)(2,1)} collective-permute-done((bf16[128,896]{0,1:T(8,128)(2,1)S(1)}, bf16[128,896]{0,1:T(8,128)(2,1)}, u32[]{:S(2)}, u32[]{:S(2)}) %collective-permute-start.4) | collective-permute-done | bytes 229408 | tf_op jit(solution)/shard_map/ppermute | solution.py:247
  52.1 4.8 %collective-permute-start.8 = (bf16[128,896]{0,1:T(8,128)(2,1)}, bf16[128,896]{0,1:T(8,128)(2,1)S(1)}, u32[]{:S(2)}, u32[]{:S(2)}) collective-permute-start(bf16[128,896]{0,1:T(8,128)(2,1)} %collective-permute-done.7), channel_id=1, source_target_pairs={{0,28},{4,0},{8,4},{12,8},{16,12},{20,16},{24,20},{28,24},{1,29},{... | collective-permute-start | bytes 688136 | tf_op jit(solution)/shard_map/ppermute | solution.py:249
  58.0 5.9 %collective-permute-done.5 = bf16[128,896]{0,1:T(8,128)(2,1)} collective-permute-done((bf16[128,896]{0,1:T(8,128)(2,1)}, bf16[128,896]{0,1:T(8,128)(2,1)}, u32[]{:S(2)}, u32[]{:S(2)}) %collective-permute-start.5) | collective-permute-done | bytes 229408 | tf_op jit(solution)/shard_map/ppermute | solution.py:247
  106.7 12.6 %collective-permute-done.10 = bf16[1,256,1024]{2,1,0:T(8,128)(2,1)S(1)} collective-permute-done((bf16[1,256,1024]{2,1,0:T(8,128)(2,1)S(1)}, bf16[1,256,1024]{2,1,0:T(8,128)(2,1)S(1)}, u32[]{:S(2)}, u32[]{:S(2)}) %collective-permute-start.10) | collective-permute-done | bytes 524320 | tf_op jit(solution)/shard_map/ppermute | solution.py:128
  121.2 11.8 %collective-permute-done.11 = bf16[1,256,1024]{2,1,0:T(8,128)(2,1)S(1)} collective-permute-done((bf16[1,256,1024]{2,1,0:T(8,128)(2,1)S(1)}, bf16[1,256,1024]{2,1,0:T(8,128)(2,1)S(1)}, u32[]{:S(2)}, u32[]{:S(2)}) %collective-permute-start.11) | collective-permute-done | bytes 524320 | tf_op jit(solution)/shard_map/ppermute | solution.py:128
  135.2 13.0 %collective-permute-done.16 = bf16[1,256,1024]{2,1,0:T(8,128)(2,1)S(1)} collective-permute-done((bf16[1,256,1024]{2,1,0:T(8,128)(2,1)S(1)}, bf16[1,256,1024]{2,1,0:T(8,128)(2,1)S(1)}, u32[]{:S(2)}, u32[]{:S(2)}) %collective-permute-start.16) | collective-permute-done | bytes 524320 | tf_op jit(solution)/shard_map/ppermute | solution.py:128
  149.5 11.6 %fusion.36 = f32[1024,2304]{1,0:T(8,128)} fusion(bf16[1024,2304]{1,0:T(8,128)(2,1)} %all-gather.3.cloned.1.call-done, bf16[1,512,1024]{2,1,0:T(8,128)(2,1)} %collective-permute-done.12, bf16[1,256,1024]{2,1,0:T(8,128)(2,1)} %copy-done.46, bf16[1,256,1024]{2,1,0:T(8,128)(2,1)S(1)} %multiply_convert_fusion.4), kind=kOutput, calls=%fused_computation.111 | convolution fusion | flops 4838129664 | bytes 16252928 | tf_op jit(solution)/shard_map/dot_general | solution.py:298
  162.8 9.3 %fusion.6 = (bf16[1024,1152]{1,0:T(8,128)(2,1)S(1)}, bf16[1024,1152]{1,0:T(8,128)(2,1)S(1)}, bf16[1024,1152]{1,0:T(8,128)(2,1)S(1)}) fusion(f32[1024,2304]{1,0:T(8,128)} %fusion.36, bf16[1024,1152]{0,1:T(8,128)(2,1)} %all-gather.5.cloned.1.call-done, bf16[1,512,1024]{2,1,0:T(8,128)(2,1)} %collective-permute-done.17, bf16[1,256,1024]{2,1,0:T(8,128)(2,1)} %copy-done.50, ...), kind=kOutput, calls=%fused_computation.18 | convolution fusion | flops 2441084928 | bytes 20971520 | tf_op jit(solution)/shard_map/dot_general | solution.py:301
  172.1 5.1 %fusion.12 = f32[1,1024,1024]{2,1,0:T(8,128)S(1)} fusion(bf16[1024,2304]{1,0:T(8,128)(2,1)S(1)} %copy-done.61, bf16[1024,1152]{1,0:T(8,128)(2,1)S(1)} %get-tuple-element.34, bf16[1024,1152]{1,0:T(8,128)(2,1)S(1)} %get-tuple-element.33), kind=kOutput, calls=%fused_computation.29 | convolution fusion | flops 4841275392 | bytes 13631488 | tf_op jit(solution)/shard_map/dot_general | solution.py:49
  182.0 12.5 %collective-permute-done.19 = bf16[1,256,1024]{2,1,0:T(8,128)(2,1)S(1)} collective-permute-done((bf16[1,256,1024]{2,1,0:T(8,128)(2,1)S(1)}, bf16[1,256,1024]{2,1,0:T(8,128)(2,1)S(1)}, u32[]{:S(2)}, u32[]{:S(2)}) %collective-permute-start.19) | collective-permute-done | bytes 524320 | tf_op jit(solution)/shard_map/ppermute | solution.py:128
  197.7 11.6 %collective-permute-done.20 = bf16[1,256,1024]{2,1,0:T(8,128)(2,1)S(1)} collective-permute-done((bf16[1,256,1024]{2,1,0:T(8,128)(2,1)S(1)}, bf16[1,256,1024]{2,1,0:T(8,128)(2,1)S(1)}, u32[]{:S(2)}, u32[]{:S(2)}) %collective-permute-start.20) | collective-permute-done | bytes 524320 | tf_op jit(solution)/shard_map/ppermute | solution.py:128
  210.6 5.6 %convolution_convert_fusion.1 = bf16[1024,1152]{1,0:T(8,128)(2,1)} fusion(bf16[1024,1152]{1,0:T(8,128)(2,1)S(1)} %get-tuple-element.35, bf16[1,512,1024]{2,1,0:T(8,128)(2,1)} %collective-permute-done.17, bf16[1,256,1024]{2,1,0:T(8,128)(2,1)S(1)} %copy-done.51, bf16[1,256,1024]{2,1,0:T(8,128)(2,1)S(1)} %copy-done.29), kind=kOutput, calls=%fused_computation.27 | convolution fusion | flops 2423390208 | bytes 6815744 | tf_op jit(solution)/shard_map/dot_general | solution.py:49
  219.2 5.5 %multiply_convert_fusion.1 = bf16[4,512,1024]{2,1,0:T(8,128)(2,1)S(1)} fusion(f32[4,512,1024]{2,1,0:T(8,128)} %copy-done.2, f32[4,512]{1,0:T(4,128)S(1)} %bitcast.214, f32[4,512]{1,0:T(4,128)S(1)} %log_add_fusion.1, pred[512,1024]{1,0:T(8,128)(4,1)S(1)} %copy-done.13, bf16[1024,4,64]{0,2,1:T(8,128)(2,1)S(1)} %bitcast.188, ...), kind=kOutput, calls=%fused_computation.1 | convolution fusion | flops 281018368 | bytes 13910016 | tf_op jit(solution)/shard_map/vmap(qhd,khd->hqk)/dot_general | solution.py:99
  235.7 3.8 fusion.22
  256.8 10.1 %convolution_convert_fusion = bf16[1024,2304]{1,0:T(8,128)(2,1)} fusion(bf16[1024,1152]{1,0:T(8,128)(2,1)} %copy-done.65, bf16[1024,1152]{1,0:T(8,128)(2,1)} %copy-done.64, bf16[1,512,1024]{2,1,0:T(8,128)(2,1)} %collective-permute-done.12, bf16[1,256,1024]{2,1,0:T(8,128)(2,1)S(1)} %copy-done.47, bf16[1,256,1024]{2,1,0:T(8,128)(2,1)S(1)} %copy-done.27), kind=kOutput, calls=%fused_computation.11 | convolution fusion | flops 4849926144 | bytes 11534336 | tf_op jit(solution)/shard_map/dot_general | solution.py:49
  266.9 5.3 %convolution_bitcast_fusion.2 = f32[1,1024,1024]{2,1,0:T(8,128)S(1)} fusion(bf16[1024,1152]{1,0:T(8,128)(2,1)} %copy-done.66, bf16[1024,1152]{0,1:T(8,128)(2,1)} %all-gather.5.cloned.1.call-done), kind=kOutput, calls=%fused_computation.32 | convolution fusion | flops 2415919104 | bytes 8912896 | tf_op jit(solution)/shard_map/dot_general | solution.py:49
  286.2 12.0 %collective-permute-done.14 = bf16[1,256,1024]{2,1,0:T(8,128)(2,1)S(1)} collective-permute-done((bf16[1,256,1024]{2,1,0:T(8,128)(2,1)S(1)}, bf16[1,256,1024]{2,1,0:T(8,128)(2,1)S(1)}, u32[]{:S(2)}, u32[]{:S(2)}) %collective-permute-start.14) | collective-permute-done | bytes 524320 | tf_op jit(solution)/shard_map/ppermute | solution.py:128
  299.4 9.5 %collective-permute-done.23 = bf16[1,256,1024]{2,1,0:T(8,128)(2,1)S(1)} collective-permute-done((bf16[1,256,1024]{2,1,0:T(8,128)(2,1)S(1)}, bf16[1,256,1024]{2,1,0:T(8,128)(2,1)S(1)}, u32[]{:S(2)}, u32[]{:S(2)}) %collective-permute-start.23) | collective-permute-done | bytes 524320 | tf_op jit(solution)/shard_map/ppermute | solution.py:128
  315.7 41.5 %psum.7 = f32[2176]{0:T(1024)S(1)} all-reduce(f32[2176]{0:T(1024)S(1)} %concatenate.109), channel_id=1, replica_groups=mesh['fsdp'=8,'ctx'=2,'tensor'=2] {'fsdp','ctx','tensor'}, use_global_device_ids=true, to_apply=%region_21.22 | all-reduce | flops 2176 | bytes 17408 | tf_op jit(solution)/shard_map/psum | solution.py:347
  373.2 78.8 %reduce-scatter.6.cloned.1.call-done = bf16[128,2304]{1,0:T(8,128)(2,1)} async-done(((bf16[1024,2304]{1,0:T(8,128)(2,1)}), bf16[128,2304]{1,0:T(8,128)(2,1)}) %reduce-scatter.6.cloned.1.call-update) | async-done | bytes 589840 | tf_op jit(solution)/shard_map/reduce_scatter | solution.py:309
  456.4 6.8 %collective-permute-done.30 = bf16[128,1152]{1,0:T(8,128)(2,1)S(1)} collective-permute-done((bf16[128,1152]{1,0:T(8,128)(2,1)S(1)}, bf16[128,1152]{1,0:T(8,128)(2,1)S(1)}, u32[]{:S(2)}, u32[]{:S(2)}) %collective-permute-start.30) | collective-permute-done | bytes 294944 | tf_op jit(solution)/shard_map/ppermute | solution.py:128
  464.4 3.8 collective-permute-done.29
  (389 shorter events, 157.9 us)
Async XLA Ops:
  7.2 142.2 %all-gather.3.cloned.1.call-start = ((), (), s32[]{:S(2)}) async-start(), calls=%async_computation.3 | async-start | bytes 5308416 | tf_op jit(solution)/shard_map/all_gather | solution.py:254
  11.8 12.8 %collective-permute-start.2 = (bf16[128,896]{0,1:T(8,128)(2,1)S(1)}, bf16[128,896]{0,1:T(8,128)(2,1)S(1)}, u32[]{:S(2)}, u32[]{:S(2)}) collective-permute-start(bf16[128,896]{0,1:T(8,128)(2,1)S(1)} %constant_dynamic-update-slice_fusion), channel_id=1, source_target_pairs={{0,4},{4,8},{8,12},{12,16},{16,20},{20,24},{24,28},{28,0},{1,5},{5... | collective-permute-start | bytes 688136 | tf_op jit(solution)/shard_map/ppermute | solution.py:247
  14.8 23.6 %collective-permute-start.6 = (bf16[128,896]{0,1:T(8,128)(2,1)S(1)}, bf16[128,896]{0,1:T(8,128)(2,1)S(1)}, u32[]{:S(2)}, u32[]{:S(2)}) collective-permute-start(bf16[128,896]{0,1:T(8,128)(2,1)S(1)} %constant_dynamic-update-slice_fusion), channel_id=1, source_target_pairs={{0,28},{4,0},{8,4},{12,8},{16,12},{20,16},{24,20},{28,24},{1,29},{... | collective-permute-start | bytes 688136 | tf_op jit(solution)/shard_map/ppermute | solution.py:249
  19.1 37.7 %collective-permute-start = (bf16[1,256,1024]{2,1,0:T(8,128)(2,1)S(1)}, bf16[1,256,1024]{2,1,0:T(8,128)(2,1)S(1)}, u32[]{:S(2)}, u32[]{:S(2)}) collective-permute-start(bf16[1,256,1024]{2,1,0:T(8,128)(2,1)S(1)} %get-tuple-element.28), channel_id=1, source_target_pairs={{0,2},{2,0},{1,3},{3,1},{4,6},{6,4},{5,7},{7,5},{8,10},{10,8},{9,1... | collective-permute-start | bytes 1572872 | tf_op jit(solution)/shard_map/ppermute | solution.py:128
  22.7 140.1 %all-gather.5.cloned.1.call-start = ((), (), s32[]{:S(2)}) async-start(), calls=%async_computation.4 | async-start | bytes 2654208 | tf_op jit(solution)/shard_map/all_gather | solution.py:255
  35.7 15.7 %collective-permute-start.4 = (bf16[128,896]{0,1:T(8,128)(2,1)S(1)}, bf16[128,896]{0,1:T(8,128)(2,1)}, u32[]{:S(2)}, u32[]{:S(2)}) collective-permute-start(bf16[128,896]{0,1:T(8,128)(2,1)S(1)} %collective-permute-done.3), channel_id=1, source_target_pairs={{0,4},{4,8},{8,12},{12,16},{16,20},{20,24},{24,28},{28,0},{1,5},{5... | collective-permute-start | bytes 688136 | tf_op jit(solution)/shard_map/ppermute | solution.py:247
  38.4 13.6 %collective-permute-start.7 = (bf16[128,896]{0,1:T(8,128)(2,1)S(1)}, bf16[128,896]{0,1:T(8,128)(2,1)}, u32[]{:S(2)}, u32[]{:S(2)}) collective-permute-start(bf16[128,896]{0,1:T(8,128)(2,1)S(1)} %collective-permute-done.6), channel_id=1, source_target_pairs={{0,28},{4,0},{8,4},{12,8},{16,12},{20,16},{24,20},{28,24},{1,29},{... | collective-permute-start | bytes 688136 | tf_op jit(solution)/shard_map/ppermute | solution.py:249
  51.5 12.4 %collective-permute-start.5 = (bf16[128,896]{0,1:T(8,128)(2,1)}, bf16[128,896]{0,1:T(8,128)(2,1)}, u32[]{:S(2)}, u32[]{:S(2)}) collective-permute-start(bf16[128,896]{0,1:T(8,128)(2,1)} %collective-permute-done.4), channel_id=1, source_target_pairs={{0,4},{4,8},{8,12},{12,16},{16,20},{20,24},{24,28},{28,0},{1,5},{5... | collective-permute-start | bytes 688136 | tf_op jit(solution)/shard_map/ppermute | solution.py:247
  52.1 16.9 %collective-permute-start.8 = (bf16[128,896]{0,1:T(8,128)(2,1)}, bf16[128,896]{0,1:T(8,128)(2,1)S(1)}, u32[]{:S(2)}, u32[]{:S(2)}) collective-permute-start(bf16[128,896]{0,1:T(8,128)(2,1)} %collective-permute-done.7), channel_id=1, source_target_pairs={{0,28},{4,0},{8,4},{12,8},{16,12},{20,16},{24,20},{28,24},{1,29},{... | collective-permute-start | bytes 688136 | tf_op jit(solution)/shard_map/ppermute | solution.py:249
  58.0 16.6 %collective-permute-start.1 = (bf16[1,512,1024]{2,1,0:T(8,128)(2,1)}, bf16[1,512,1024]{2,1,0:T(8,128)(2,1)}, u32[]{:S(2)}, u32[]{:S(2)}) collective-permute-start(bf16[1,512,1024]{2,1,0:T(8,128)(2,1)} %pad_maximum_fusion.6), channel_id=1, source_target_pairs={{0,1},{1,0},{2,3},{3,2},{4,5},{5,4},{6,7},{7,6},{8,9},{9,8},{10,11... | collective-permute-start | bytes 3145736 | tf_op jit(solution)/shard_map/ppermute | solution.py:128
  101.2 211.7 %reduce-scatter.8.cloned.1.call-start = ((), (), s32[]{:S(2)}) async-start(), calls=%async_computation.6 | async-start | bytes 2654208 | tf_op jit(solution)/shard_map/reduce_scatter | solution.py:307
  105.3 14.0 %collective-permute-start.10 = (bf16[1,256,1024]{2,1,0:T(8,128)(2,1)S(1)}, bf16[1,256,1024]{2,1,0:T(8,128)(2,1)S(1)}, u32[]{:S(2)}, u32[]{:S(2)}) collective-permute-start(bf16[1,256,1024]{2,1,0:T(8,128)(2,1)S(1)} %slice.347), channel_id=1, source_target_pairs={{0,2},{2,0},{1,3},{3,1},{4,6},{6,4},{5,7},{7,5},{8,10},{10,8},{9,1... | collective-permute-start | bytes 1572872 | tf_op jit(solution)/shard_map/ppermute | solution.py:128
  119.8 13.2 %collective-permute-start.11 = (bf16[1,256,1024]{2,1,0:T(8,128)(2,1)S(1)}, bf16[1,256,1024]{2,1,0:T(8,128)(2,1)S(1)}, u32[]{:S(2)}, u32[]{:S(2)}) collective-permute-start(bf16[1,256,1024]{2,1,0:T(8,128)(2,1)S(1)} %multiply_convert_fusion.4), channel_id=1, source_target_pairs={{0,2},{2,0},{1,3},{3,1},{4,6},{6,4},{5,7},{7,5},{8,10},{10,8},{9,1... | collective-permute-start | bytes 1572872 | tf_op jit(solution)/shard_map/ppermute | solution.py:128
  133.8 15.7 %collective-permute-start.12 = (bf16[1,512,1024]{2,1,0:T(8,128)(2,1)S(1)}, bf16[1,512,1024]{2,1,0:T(8,128)(2,1)}, u32[]{:S(2)}, u32[]{:S(2)}) collective-permute-start(bf16[1,512,1024]{2,1,0:T(8,128)(2,1)S(1)} %pad_maximum_fusion.7), channel_id=1, source_target_pairs={{0,1},{1,0},{2,3},{3,2},{4,5},{5,4},{6,7},{7,6},{8,9},{9,8},{10,11... | collective-permute-start | bytes 3145736 | tf_op jit(solution)/shard_map/ppermute | solution.py:128
  133.8 14.4 %collective-permute-start.16 = (bf16[1,256,1024]{2,1,0:T(8,128)(2,1)S(1)}, bf16[1,256,1024]{2,1,0:T(8,128)(2,1)S(1)}, u32[]{:S(2)}, u32[]{:S(2)}) collective-permute-start(bf16[1,256,1024]{2,1,0:T(8,128)(2,1)S(1)} %constant_dynamic-slice_fusion), channel_id=1, source_target_pairs={{0,2},{2,0},{1,3},{3,1},{4,6},{6,4},{5,7},{7,5},{8,10},{10,8},{9,1... | collective-permute-start | bytes 1572872 | tf_op jit(solution)/shard_map/ppermute | solution.py:128
  180.5 14.0 %collective-permute-start.19 = (bf16[1,256,1024]{2,1,0:T(8,128)(2,1)S(1)}, bf16[1,256,1024]{2,1,0:T(8,128)(2,1)S(1)}, u32[]{:S(2)}, u32[]{:S(2)}) collective-permute-start(bf16[1,256,1024]{2,1,0:T(8,128)(2,1)S(1)} %slice.345), channel_id=1, source_target_pairs={{0,2},{2,0},{1,3},{3,1},{4,6},{6,4},{5,7},{7,5},{8,10},{10,8},{9,1... | collective-permute-start | bytes 1572872 | tf_op jit(solution)/shard_map/ppermute | solution.py:128
  196.2 13.1 %collective-permute-start.20 = (bf16[1,256,1024]{2,1,0:T(8,128)(2,1)S(1)}, bf16[1,256,1024]{2,1,0:T(8,128)(2,1)S(1)}, u32[]{:S(2)}, u32[]{:S(2)}) collective-permute-start(bf16[1,256,1024]{2,1,0:T(8,128)(2,1)S(1)} %get-tuple-element.25), channel_id=1, source_target_pairs={{0,2},{2,0},{1,3},{3,1},{4,6},{6,4},{5,7},{7,5},{8,10},{10,8},{9,1... | collective-permute-start | bytes 1572872 | tf_op jit(solution)/shard_map/ppermute | solution.py:128
  216.3 144.9 %reduce-scatter.10.cloned.1.call-start = ((), (), s32[]{:S(2)}) async-start(), calls=%async_computation.7 | async-start | bytes 1769472
  256.5 195.5 %reduce-scatter.6.cloned.1.call-start = ((), (), s32[]{:S(2)}) async-start(), calls=%async_computation.5 | async-start | bytes 5308416 | tf_op jit(solution)/shard_map/reduce_scatter | solution.py:309
  283.3 14.9 %collective-permute-start.14 = (bf16[1,256,1024]{2,1,0:T(8,128)(2,1)S(1)}, bf16[1,256,1024]{2,1,0:T(8,128)(2,1)S(1)}, u32[]{:S(2)}, u32[]{:S(2)}) collective-permute-start(bf16[1,256,1024]{2,1,0:T(8,128)(2,1)S(1)} %slice.346), channel_id=1, source_target_pairs={{0,2},{2,0},{1,3},{3,1},{4,6},{6,4},{5,7},{7,5},{8,10},{10,8},{9,1... | collective-permute-start | bytes 1572872 | tf_op jit(solution)/shard_map/ppermute | solution.py:128
  285.4 23.5 %collective-permute-start.23 = (bf16[1,256,1024]{2,1,0:T(8,128)(2,1)S(1)}, bf16[1,256,1024]{2,1,0:T(8,128)(2,1)S(1)}, u32[]{:S(2)}, u32[]{:S(2)}) collective-permute-start(bf16[1,256,1024]{2,1,0:T(8,128)(2,1)S(1)} %slice.344), channel_id=1, source_target_pairs={{0,2},{2,0},{1,3},{3,1},{4,6},{6,4},{5,7},{7,5},{8,10},{10,8},{9,1... | collective-permute-start | bytes 1572872 | tf_op jit(solution)/shard_map/ppermute | solution.py:128
  311.0 48.8 %collective-permute-start.24 = (f32[1,256,1024]{2,1,0:T(8,128)}, f32[1,256,1024]{2,1,0:T(8,128)}, u32[]{:S(2)}, u32[]{:S(2)}) collective-permute-start(f32[1,256,1024]{2,1,0:T(8,128)} %get-tuple-element.24), channel_id=1, source_target_pairs={{0,1},{1,0},{2,3},{3,2},{4,5},{5,4},{6,7},{7,6},{8,9},{9,8},{10,11... | collective-permute-start | bytes 3145736 | tf_op jit(solution)/shard_map/ppermute | solution.py:128
  314.1 44.4 %collective-permute-start.31 = (bf16[1152,128]{0,1:T(8,128)(2,1)}, bf16[1152,128]{0,1:T(8,128)(2,1)S(1)}, u32[]{:S(2)}, u32[]{:S(2)}) collective-permute-start(bf16[1152,128]{0,1:T(8,128)(2,1)} %bitcast.198), channel_id=1, source_target_pairs={{0,2},{2,0},{1,3},{3,1},{4,6},{6,4},{5,7},{7,5},{8,10},{10,8},{9,1... | collective-permute-start | bytes 884744 | tf_op jit(solution)/shard_map/ppermute | solution.py:128
  454.8 13.3 %collective-permute-start.29 = (bf16[128,1152]{1,0:T(8,128)(2,1)S(1)}, bf16[128,1152]{1,0:T(8,128)(2,1)S(1)}, u32[]{:S(2)}, u32[]{:S(2)}) collective-permute-start(bf16[128,1152]{1,0:T(8,128)(2,1)S(1)} %get-tuple-element.46), channel_id=1, source_target_pairs={{0,2},{2,0},{1,3},{3,1},{4,6},{6,4},{5,7},{7,5},{8,10},{10,8},{9,1... | collective-permute-start | bytes 884744 | tf_op jit(solution)/shard_map/ppermute | solution.py:128
  (86 other events, 920.5 us)
Sparse Core Ops, SparseCore 0:
  22.8 86.2 all-gather.2
  111.1 51.6 all-gather.4
  216.4 69.2 reduce-scatter.7
  289.0 64.9 reduce-scatter.9
  357.5 94.5 reduce-scatter.5
